TPU v7x, 32 devices: a whole 2x2x4 slice. The times are simulated.
32 devices in a mesh: dp: 4 (over y, core), fsdp: 8 (over z, x).
Axes of the slice: x: 2, y: 2, z: 4, core: 2. Of those that a mesh axis runs over, the one named last changes fastest.
Arguments:
- latents: int32 [256, 64, 32], P(('dp', 'fsdp')), may hold values from 0 to 31
- actions: int32 [256, 64], P(('dp', 'fsdp')), may hold values from 0 to 17, as said below
- game_ids: int32 [256], P(('dp', 'fsdp')), may hold values from 0 to 25
- action_masks: int32 [26, 18], replicated, may hold values from 0 to 1, as said below
- valid_steps: int32 [256, 64], P(('dp', 'fsdp')), may hold values from 0 to 1, as said below
- target_bins: int32 [256, 64, 2], P(('dp', 'fsdp')), may hold values from 0 to 253
- target_fracs: float32 [256, 64, 2], P(('dp', 'fsdp')), may hold values from 0 to 1
- continues: int32 [256, 64], P(('dp', 'fsdp')), may hold values 0 or 1
- owner_order: int32 [192], replicated, may hold values from 0 to 191, each once
- blocks: float32 [192, 128, 128], P('fsdp'), may hold values from -0.25 to 0.25
- block_first: float32 [192, 128, 128], P('fsdp'), may hold values from -1.5258789e-05 to 1.5258789e-05
- block_second: float32 [192, 128, 128], P('fsdp'), may hold values from 5.649883e-12 to 2.2554868e-11
- left_stat: float32 [192, 128, 128], P('fsdp'), may hold values from -2.85843873e-09 to 2.9156075e-09, as said below
- right_stat: float32 [192, 128, 128], P('fsdp'), may hold values from -2.85843873e-09 to 2.9156075e-09, as said below
- left_basis: float32 [192, 128, 128], P('fsdp'), may hold values from -1 to 1, as said below
- right_basis: float32 [192, 128, 128], P('fsdp'), may hold values from -1 to 1, as said below
- latent_maps: float32 [2048, 512], P('fsdp'), may hold values from -0.625 to 0.625
- latent_first: float32 [2048, 512], P('fsdp'), may hold values from -1.5258789e-05 to 1.5258789e-05
- latent_second: float32 [2048, 512], P('fsdp'), may hold values from 5.649883e-12 to 2.2554868e-11
- head_weights: float32 [513, 529], replicated, may hold values from -0.625 to 0.625
- head_first: float32 [513, 529], replicated, may hold values from -1.5258789e-05 to 1.5258789e-05
- head_second: float32 [513, 529], replicated, may hold values from 5.649883e-12 to 2.2554868e-11
- small_params: float32 [24, 512], replicated
- small_first: float32 [24, 512], replicated, may hold values from -1.5258789e-05 to 1.5258789e-05
- small_second: float32 [24, 512], replicated, may hold values from 5.649883e-12 to 2.2554868e-11
- ema_critic: float32 [513, 255], replicated, may hold values from -0.15625 to 0.15625
Outputs:
- loss: float32 [], replicated
- grad_norm: float32 [], replicated
- blocks_new: float32 [192, 128, 128], P('fsdp')
- block_first_new: float32 [192, 128, 128], P('fsdp')
- block_second_new: float32 [192, 128, 128], P('fsdp')
- left_stat_new: float32 [192, 128, 128], P('fsdp')
- right_stat_new: float32 [192, 128, 128], P('fsdp')
- left_basis_new: float32 [192, 128, 128], P('fsdp')
- right_basis_new: float32 [192, 128, 128], P('fsdp')
- latent_maps_new: float32 [2048, 512], P('fsdp')
- latent_first_new: float32 [2048, 512], P('fsdp')
- latent_second_new: float32 [2048, 512], P('fsdp')
- head_weights_new: float32 [513, 529], replicated
- head_first_new: float32 [513, 529], replicated
- head_second_new: float32 [513, 529], replicated
- small_params_new: float32 [24, 512], replicated
- small_first_new: float32 [24, 512], replicated
- small_second_new: float32 [24, 512], replicated
- ema_critic_new: float32 [513, 255], replicated
Inputs may be any that keep to these rules, and one draw needn't show every extreme that they name: `actions`: every action is legal in its sequence's game. `action_masks`: every game allows action 0. `valid_steps`: each sequence is 1 on a prefix of 16 frames or more and 0 after it. `owner_order`: a permutation of the blocks. `left_stat`: symmetric positive definite. `right_stat`: symmetric positive definite. `left_basis`: orthogonal. `right_basis`: orthogonal.
All inputs are finite; a program needn't handle non-finite values. Where the computation divides by a largest or mean magnitude, that divisor is 1e-20 or more. No bound on the sum of `continues` on one device may be relied on, other than what follows from the above.
Results may differ from a plain program's by a relative error of at most 0.0053.
Values may be sent and summed in bfloat16 or wider, within the bound.
No kernel may reach another device: no remote copies, remote signals or barrier semaphores. Data moves between devices by JAX's collectives and lax.ppermute only.
A program may use at most 192 MiB of HBM per device.

v0:
```python
import math

import jax
import jax.numpy as jnp
from jax import lax
from jax.sharding import PartitionSpec as P

D = 512
NH = 8
DH = 64
FF = 2048
GROUPS = 32
CLASSES = 32
LAT = 1024
BINS = 255
NA = 18
LAYERS = 1
F = 64
NGAME = 26
BS = 128
STEP = 10


HIGHEST = lax.Precision.HIGHEST
beta_one = 0.9
beta_two = 0.99
epsilon = 1e-08
learn_rate = 0.03
small_rate = 0.15
weight_decay = 0.01
clip_norm = 0.05
ema_rate = 0.98
norm_eps = 1e-05


def dot_rows(left_op, right_op):
    return lax.dot_general(
        left_op, right_op, (((1,), (1,)), ((), ())), preferred_element_type=jnp.float32
    )


def dot_cols(left_op, right_op):
    return lax.dot_general(
        left_op, right_op, (((0,), (0,)), ((), ())), preferred_element_type=jnp.float32
    )


def from_blocks(pieces, block_rows, block_cols):
    side = pieces.shape[-1]
    return (
        pieces.reshape(block_rows, block_cols, side, side)
        .transpose(0, 2, 1, 3)
        .reshape(block_rows * side, block_cols * side)
    )


def to_blocks(matrix):
    block_rows = matrix.shape[0] // BS
    block_cols = matrix.shape[1] // BS
    return (
        matrix.reshape(block_rows, BS, block_cols, BS)
        .transpose(0, 2, 1, 3)
        .reshape(block_rows * block_cols, BS, BS)
    )


def layer_mats(block_ids):
    tile_count = D // BS
    wide_count = FF // BS
    first_end = 3 * tile_count * tile_count
    second_end = first_end + tile_count * tile_count
    third_end = second_end + tile_count * wide_count
    joint_map = from_blocks(block_ids[:first_end], tile_count, 3 * tile_count)
    output_map = from_blocks(block_ids[first_end:second_end], tile_count, tile_count)
    expand = from_blocks(block_ids[second_end:third_end], tile_count, wide_count)
    contract = from_blocks(block_ids[third_end:], wide_count, tile_count)
    return (joint_map, output_map, expand, contract)


def positions(frames, width):
    frame_index = jnp.arange(frames).astype(jnp.float32)[:, None]
    feature = jnp.arange(width)
    freq = jnp.exp(-(feature // 2 * 2).astype(jnp.float32) * (math.log(10000.0) / width))
    angle = frame_index * freq[None, :]
    return jnp.where(feature % 2 == 0, jnp.sin(angle), jnp.cos(angle))


def norm_forward(inputs, gain_row, bias_row):
    center = inputs - jnp.mean(inputs, -1, keepdims=True)
    rstd_value = lax.rsqrt(jnp.mean(center * center, -1, keepdims=True) + norm_eps)
    scaled = center * rstd_value
    return (scaled * gain_row + bias_row, scaled, rstd_value)


def norm_backward(grad_out, scaled, rstd_value, gain_row):
    grad_scaled = grad_out * gain_row
    grad_in = rstd_value * (
        grad_scaled
        - jnp.mean(grad_scaled, -1, keepdims=True)
        - scaled * jnp.mean(grad_scaled * scaled, -1, keepdims=True)
    )
    return (grad_in, jnp.sum(grad_out * scaled, 0), jnp.sum(grad_out, 0))


def split_heads(qkv_low, seqs_here):
    shaped = qkv_low.reshape(seqs_here, F, 3, NH, DH)
    return (shaped[:, :, 0], shaped[:, :, 1], shaped[:, :, 2])


def attention_scores(queries, keys_all):
    scores = jnp.einsum(
        "sqhd,skhd->shqk", queries, keys_all, preferred_element_type=jnp.float32
    ) * DH ** (-0.5)
    causal = jnp.arange(F)[:, None] >= jnp.arange(F)[None, :]
    return jnp.where(causal, scores, -1e30)


def layer_forward(hidden, matrices, gains, seqs_here):
    joint_map, output_map, expand, contract = matrices
    normed, scaled_one, rstd_one = norm_forward(hidden, gains[0], gains[1])
    normed_low = normed.astype(jnp.bfloat16)
    qkv_low = jnp.dot(normed_low, joint_map, preferred_element_type=jnp.float32).astype(
        jnp.bfloat16
    )
    queries, keys_all, values_all = split_heads(qkv_low, seqs_here)
    scores = attention_scores(queries, keys_all)
    lse_value = jax.nn.logsumexp(scores, -1, keepdims=True)
    attn_probs = jnp.exp(scores - lse_value)
    mixed_out = jnp.einsum(
        "shqk,skhd->sqhd",
        attn_probs.astype(jnp.bfloat16),
        values_all,
        preferred_element_type=jnp.float32,
    )
    mixed_low = mixed_out.astype(jnp.bfloat16).reshape(-1, D)
    middle = hidden + jnp.dot(mixed_low, output_map, preferred_element_type=jnp.float32)
    normed_two, scaled_two, rstd_two = norm_forward(middle, gains[2], gains[3])
    normed_two_low = normed_two.astype(jnp.bfloat16)
    pre_act = jnp.dot(normed_two_low, expand, preferred_element_type=jnp.float32)
    act_low = jax.nn.gelu(pre_act, approximate=True).astype(jnp.bfloat16)
    output = middle + jnp.dot(act_low, contract, preferred_element_type=jnp.float32)
    kept_state = (
        scaled_one,
        rstd_one,
        normed_low,
        qkv_low,
        lse_value,
        mixed_low,
        scaled_two,
        rstd_two,
        normed_two_low,
        pre_act,
        act_low,
    )
    return (output, kept_state)


def layer_backward(grad_out, matrices, gains, kept_state, seqs_here):
    joint_map, output_map, expand, contract = matrices
    (
        scaled_one,
        rstd_one,
        normed_low,
        qkv_low,
        lse_value,
        mixed_low,
        scaled_two,
        rstd_two,
        normed_two_low,
        pre_act,
        act_low,
    ) = kept_state
    grad_low = grad_out.astype(jnp.bfloat16)
    grad_contract = dot_cols(act_low, grad_low)
    grad_act = dot_rows(grad_low, contract)
    _, gelu_pull = jax.vjp(lambda value: jax.nn.gelu(value, approximate=True), pre_act)
    grad_pre = gelu_pull(grad_act)[0].astype(jnp.bfloat16)
    grad_expand = dot_cols(normed_two_low, grad_pre)
    grad_normed_two = dot_rows(grad_pre, expand)
    grad_from_two, gain_two, bias_two = norm_backward(
        grad_normed_two, scaled_two, rstd_two, gains[2]
    )
    grad_middle = grad_out + grad_from_two
    grad_mid_low = grad_middle.astype(jnp.bfloat16)
    grad_output_map = dot_cols(mixed_low, grad_mid_low)
    grad_mixed = (
        dot_rows(grad_mid_low, output_map).astype(jnp.bfloat16).reshape(seqs_here, F, NH, DH)
    )
    queries, keys_all, values_all = split_heads(qkv_low, seqs_here)
    attn_probs = jnp.exp(attention_scores(queries, keys_all) - lse_value)
    grad_values = jnp.einsum(
        "shqk,sqhd->skhd",
        attn_probs.astype(jnp.bfloat16),
        grad_mixed,
        preferred_element_type=jnp.float32,
    )
    grad_probs = jnp.einsum(
        "sqhd,skhd->shqk", grad_mixed, values_all, preferred_element_type=jnp.float32
    )
    grad_scores = (
        attn_probs * (grad_probs - jnp.sum(grad_probs * attn_probs, -1, keepdims=True))
    ).astype(jnp.bfloat16)
    grad_queries = jnp.einsum(
        "shqk,skhd->sqhd", grad_scores, keys_all, preferred_element_type=jnp.float32
    ) * DH ** (-0.5)
    grad_keys = jnp.einsum(
        "shqk,sqhd->skhd", grad_scores, queries, preferred_element_type=jnp.float32
    ) * DH ** (-0.5)
    grad_qkv = (
        jnp.stack([grad_queries, grad_keys, grad_values], 2).reshape(-1, 3 * D).astype(jnp.bfloat16)
    )
    grad_joint = dot_cols(normed_low, grad_qkv)
    grad_normed = dot_rows(grad_qkv, joint_map)
    grad_from_one, gain_one, bias_one = norm_backward(grad_normed, scaled_one, rstd_one, gains[0])
    gain_grads = jnp.stack([gain_one, bias_one, gain_two, bias_two], 0)
    return (
        grad_middle + grad_from_one,
        (grad_joint, grad_output_map, grad_expand, grad_contract),
        gain_grads,
    )


def two_hot_terms(logits, lower_bin, upper_frac):
    bin_index = jnp.arange(logits.shape[-1])
    weights = jnp.where(bin_index == lower_bin[:, None], 1.0 - upper_frac[:, None], 0.0)
    weights = weights + jnp.where(bin_index == lower_bin[:, None] + 1, upper_frac[:, None], 0.0)
    log_probs = jax.nn.log_softmax(logits, -1)
    return (-jnp.sum(log_probs * weights, -1), jnp.exp(log_probs) - weights)


def renew(stat, basis):
    scale = jnp.max(jnp.sum(jnp.abs(stat), -1), -1)[:, None, None]
    iterate = jnp.einsum("bij,bjk->bik", stat, basis, precision=HIGHEST) / scale
    gram = jnp.einsum("bji,bjk->bik", iterate, iterate, precision=HIGHEST)
    lower_factor = jnp.linalg.cholesky(gram)
    solved = jax.scipy.linalg.solve_triangular(
        lower_factor, jnp.swapaxes(iterate, 1, 2), lower=True
    )
    return jnp.swapaxes(solved, 1, 2)


def soap_update(weight, first_moment, second_moment, left, right, left_rot, right_rot, grad):
    left = beta_two * left + (1.0 - beta_two) * jnp.einsum(
        "bij,bkj->bik", grad, grad, precision=HIGHEST
    )
    right = beta_two * right + (1.0 - beta_two) * jnp.einsum(
        "bji,bjk->bik", grad, grad, precision=HIGHEST
    )
    rotated = jnp.einsum("bji,bjk->bik", left_rot, grad, precision=HIGHEST)
    rotated = jnp.einsum("bij,bjk->bik", rotated, right_rot, precision=HIGHEST)
    first_moment = beta_one * first_moment + (1.0 - beta_one) * rotated
    second_moment = beta_two * second_moment + (1.0 - beta_two) * rotated * rotated
    direction = (
        first_moment
        / (1.0 - beta_one**STEP)
        / (jnp.sqrt(second_moment / (1.0 - beta_two**STEP)) + epsilon)
    )
    direction = jnp.einsum("bij,bjk->bik", left_rot, direction, precision=HIGHEST)
    direction = jnp.einsum("bij,bkj->bik", direction, right_rot, precision=HIGHEST)
    weight = weight - learn_rate * (direction + weight_decay * weight)
    return (
        weight,
        first_moment,
        second_moment,
        left,
        right,
        renew(left, left_rot),
        renew(right, right_rot),
    )


def adam_update(weight, first_moment, second_moment, grad, decay_rate, rate):
    first_moment = beta_one * first_moment + (1.0 - beta_one) * grad
    second_moment = beta_two * second_moment + (1.0 - beta_two) * grad * grad
    direction = (
        first_moment
        / (1.0 - beta_one**STEP)
        / (jnp.sqrt(second_moment / (1.0 - beta_two**STEP)) + epsilon)
    )
    return (weight - rate * (direction + decay_rate * weight), first_moment, second_moment)


def shards(
    latents,
    actions,
    game_ids,
    action_masks,
    valid_steps,
    target_bins,
    target_fracs,
    continues,
    owner_order,
    blocks,
    block_first,
    block_second,
    left_stat,
    right_stat,
    left_basis,
    right_basis,
    latent_maps,
    latent_first,
    latent_second,
    head_weights,
    head_first,
    head_second,
    small_params,
    small_first,
    small_second,
    ema_critic,
):
    seqs_here = latents.shape[0]
    tokens = seqs_here * F
    counted = lax.psum(jnp.sum(valid_steps.astype(jnp.float32)), ("dp", "fsdp"))
    shard_low = (blocks.astype(jnp.bfloat16), latent_maps.astype(jnp.bfloat16))
    slots_all, maps_all = (
        lax.all_gather(shard_low[0], "fsdp", axis=0, tiled=True),
        lax.all_gather(shard_low[1], "fsdp", axis=0, tiled=True),
    )
    inverse = jnp.argsort(owner_order)
    ids_all = slots_all[inverse]
    latent_hot = (
        jnp.repeat(latents.reshape(tokens, GROUPS), CLASSES, axis=1)
        == jnp.tile(jnp.arange(CLASSES), GROUPS)[None, :]
    ).astype(jnp.bfloat16)
    action_hot = (actions.reshape(tokens, 1) == jnp.arange(NA)[None, :]).astype(jnp.float32)
    hidden = jnp.dot(latent_hot, maps_all[:LAT], preferred_element_type=jnp.float32)
    hidden = hidden + jnp.dot(action_hot, small_params[4 * LAYERS + 2 :], precision=HIGHEST)
    hidden = (hidden.reshape(seqs_here, F, D) + positions(F, D)[None]).reshape(tokens, D)
    layer_index = 0
    matrices = layer_mats(ids_all)
    hidden, kept_state = layer_forward(
        hidden, matrices, small_params[4 * layer_index : 4 * layer_index + 4], seqs_here
    )
    states_kept = [kept_state]
    final_norm, final_scaled, final_rstd = norm_forward(
        hidden, small_params[4 * LAYERS], small_params[4 * LAYERS + 1]
    )
    final_low = final_norm.astype(jnp.bfloat16)
    dyn_logits = dot_rows(final_low, maps_all[LAT:]).reshape(tokens, GROUPS, CLASSES)
    head_low = head_weights[:D].astype(jnp.bfloat16)
    head_out = jnp.dot(final_low, head_low, preferred_element_type=jnp.float32) + head_weights[D]
    frame_last = (jnp.arange(F) < F - 1).astype(jnp.float32)[None, :]
    later = (jnp.roll(valid_steps, -1, axis=1).astype(jnp.float32) * frame_last).reshape(tokens)
    now = valid_steps.astype(jnp.float32).reshape(tokens)
    next_latent = jnp.roll(latents, -1, axis=1).reshape(tokens, GROUPS, 1)
    dyn_target = (next_latent == jnp.arange(CLASSES)).astype(jnp.float32)
    dyn_log = jax.nn.log_softmax(dyn_logits, -1)
    dyn_loss = -jnp.sum(jnp.sum(dyn_log * dyn_target, (1, 2)) * later)
    grad_dyn = (
        ((jnp.exp(dyn_log) - dyn_target) * (later / counted)[:, None, None])
        .reshape(tokens, LAT)
        .astype(jnp.bfloat16)
    )
    bins_flat = target_bins.reshape(tokens, 2)
    fracs_flat = target_fracs.reshape(tokens, 2)
    reward_loss, reward_grad = two_hot_terms(head_out[:, :BINS], bins_flat[:, 0], fracs_flat[:, 0])
    critic_loss, critic_grad = two_hot_terms(
        head_out[:, BINS : 2 * BINS], bins_flat[:, 1], fracs_flat[:, 1]
    )
    cont_logit = head_out[:, 2 * BINS]
    cont_target = continues.reshape(tokens).astype(jnp.float32)
    cont_loss = jax.nn.softplus(cont_logit) - cont_target * cont_logit
    cont_grad = jax.nn.sigmoid(cont_logit) - cont_target
    game_hot = (game_ids[:, None] == jnp.arange(NGAME)[None, :]).astype(jnp.float32)
    legal_rows = jnp.dot(game_hot, action_masks.astype(jnp.float32), precision=HIGHEST)
    legal_tok = (
        jnp.broadcast_to(legal_rows[:, None, :], (seqs_here, F, NA)).reshape(tokens, NA) > 0.5
    )
    masked = jnp.where(legal_tok, head_out[:, 2 * BINS + 1 :], -1e30)
    actor_log = jax.nn.log_softmax(masked, -1)
    next_action = (
        jnp.roll(actions, -1, axis=1).reshape(tokens, 1) == jnp.arange(NA)[None, :]
    ).astype(jnp.float32)
    actor_loss = -jnp.sum(jnp.sum(actor_log * next_action, -1) * later)
    loss_local = (
        dyn_loss + actor_loss + jnp.sum((reward_loss + critic_loss + cont_loss) * now)
    ) / counted
    grad_head = jnp.concatenate(
        [
            reward_grad * now[:, None],
            critic_grad * now[:, None],
            (cont_grad * now)[:, None],
            (jnp.exp(actor_log) - next_action) * later[:, None],
        ],
        1,
    )
    grad_head = (grad_head / counted).astype(jnp.bfloat16)
    back_slots, back_maps = (
        lax.all_gather(shard_low[0], "fsdp", axis=0, tiled=True),
        lax.all_gather(shard_low[1], "fsdp", axis=0, tiled=True),
    )
    back_ids = back_slots[inverse]
    grad_dyn_table = dot_cols(grad_dyn, final_low)
    grad_head_matrix = dot_cols(final_low, grad_head)
    grad_head_bias = jnp.sum(grad_head.astype(jnp.float32), 0)
    grad_final = jnp.dot(grad_dyn, back_maps[LAT:], preferred_element_type=jnp.float32) + dot_rows(
        grad_head, head_low
    )
    grad_hidden, final_gain, final_bias = norm_backward(
        grad_final, final_scaled, final_rstd, small_params[4 * LAYERS]
    )
    block_parts = [None] * LAYERS
    small_parts = [None] * LAYERS
    for layer_index in reversed(range(LAYERS)):
        matrices = layer_mats(back_ids)
        grad_hidden, matrix_grads, gain_grads = layer_backward(
            grad_hidden,
            matrices,
            small_params[4 * layer_index : 4 * layer_index + 4],
            states_kept[layer_index],
            seqs_here,
        )
        block_parts[layer_index] = jnp.concatenate([to_blocks(piece) for piece in matrix_grads], 0)
        small_parts[layer_index] = gain_grads
    grad_lat_table = dot_cols(latent_hot, grad_hidden.astype(jnp.bfloat16))
    grad_act_table = lax.dot_general(
        action_hot, grad_hidden, (((0,), (0,)), ((), ())), precision=HIGHEST
    )
    grad_ids = block_parts[0]
    grad_slots = grad_ids[owner_order]
    grad_maps = jnp.concatenate([grad_lat_table, grad_dyn_table], 0)
    small_local = jnp.concatenate(
        small_parts + [final_gain[None], final_bias[None], grad_act_table], 0
    )
    head_local = jnp.concatenate([grad_head_matrix, grad_head_bias[None]], 0)
    shard_grads = (
        lax.psum_scatter(grad_slots, "fsdp", scatter_dimension=0, tiled=True),
        lax.psum_scatter(grad_maps, "fsdp", scatter_dimension=0, tiled=True),
    )
    block_grad, maps_grad = lax.psum((shard_grads[0], shard_grads[1]), "dp")
    head_grad, small_grad, loss_value = lax.psum(
        (head_local, small_local, loss_local), ("dp", "fsdp")
    )
    held_square = lax.psum(
        jnp.sum(block_grad * block_grad) + jnp.sum(maps_grad * maps_grad), "fsdp"
    )
    grad_norm = jnp.sqrt(
        held_square + jnp.sum(head_grad * head_grad) + jnp.sum(small_grad * small_grad)
    )
    factor = jnp.minimum(1.0, clip_norm / grad_norm)
    soap_out = soap_update(
        blocks,
        block_first,
        block_second,
        left_stat,
        right_stat,
        left_basis,
        right_basis,
        block_grad * factor,
    )
    maps_out = adam_update(
        latent_maps, latent_first, latent_second, maps_grad * factor, weight_decay, learn_rate
    )
    heads_out = adam_update(
        head_weights, head_first, head_second, head_grad * factor, weight_decay, learn_rate
    )
    small_out = adam_update(
        small_params, small_first, small_second, small_grad * factor, 0.0, small_rate
    )
    ema_new = ema_rate * ema_critic + (1.0 - ema_rate) * heads_out[0][:, BINS : 2 * BINS]
    return (
        loss_value,
        grad_norm,
        soap_out[0],
        soap_out[1],
        soap_out[2],
        soap_out[3],
        soap_out[4],
        soap_out[5],
        soap_out[6],
        maps_out[0],
        maps_out[1],
        maps_out[2],
        heads_out[0],
        heads_out[1],
        heads_out[2],
        small_out[0],
        small_out[1],
        small_out[2],
        ema_new,
    )


def solution(mesh):
    placed = (
        P(("dp", "fsdp"), None, None),
        P(("dp", "fsdp"), None),
        P(("dp", "fsdp")),
        P(),
        P(("dp", "fsdp"), None),
        P(("dp", "fsdp"), None, None),
        P(("dp", "fsdp"), None, None),
        P(("dp", "fsdp"), None),
        P(),
        P("fsdp", None, None),
        P("fsdp", None, None),
        P("fsdp", None, None),
        P("fsdp", None, None),
        P("fsdp", None, None),
        P("fsdp", None, None),
        P("fsdp", None, None),
        P("fsdp", None),
        P("fsdp", None),
        P("fsdp", None),
        P(),
        P(),
        P(),
        P(),
        P(),
        P(),
        P(),
    )
    return jax.shard_map(
        shards,
        mesh=mesh,
        in_specs=placed,
        out_specs=(
            P(),
            P(),
            P("fsdp", None, None),
            P("fsdp", None, None),
            P("fsdp", None, None),
            P("fsdp", None, None),
            P("fsdp", None, None),
            P("fsdp", None, None),
            P("fsdp", None, None),
            P("fsdp", None),
            P("fsdp", None),
            P("fsdp", None),
            P(),
            P(),
            P(),
            P(),
            P(),
            P(),
            P(),
        ),
        check_vma=False,
    )
```

profile of v0, /device:TPU:0, one launch (start us, length us, event | category | flops | bytes accessed | tf_op | source)
XLA Modules:
  0.0 2004.8 jit_solution(17724890745297580318)
XLA Ops:
  16.8 2.9 copy.283
  22.2 2.9 copy.281
  25.1 3.2 sort.17
  31.0 31.7 %all-gather.3.cloned.1.call-done = bf16[2048,512]{1,0:T(8,128)(2,1)} async-done(((bf16[256,512]{1,0:T(8,128)(2,1)}), bf16[2048,512]{1,0:T(8,128)(2,1)}) %all-gather.3.cloned.1.call-update) | async-done | bytes 2097168 | tf_op jit(solution)/shard_map/all_gather | solution.py:317
  66.1 96.7 %all-gather.5.cloned.1.call-done = bf16[192,128,128]{2,1,0:T(8,128)(2,1)} async-done(((bf16[24,128,128]{2,1,0:T(8,128)(2,1)}), bf16[192,128,128]{2,1,0:T(8,128)(2,1)}) %all-gather.5.cloned.1.call-update) | async-done | bytes 6291472 | tf_op jit(solution)/shard_map/all_gather | solution.py:316
  162.7 10.8 gather_fusion
  176.3 4.7 fusion.136
  181.0 3.7 copy.285
  184.8 3.6 convolution_convert_fusion
  188.4 5.1 reshape.392
  193.4 3.6 fusion.137
  207.5 2.7 reshape.393
  211.5 4.5 copy.293
  216.0 3.0 copy.292
  229.7 39.0 %psum.49 = f32[]{:T(128)} all-reduce(f32[]{:T(128)} %get-tuple-element.136), channel_id=1, replica_groups=mesh['dp'=4,'fsdp'=8] {'dp','fsdp'}, use_global_device_ids=true, to_apply=%region_23.25 | all-reduce | flops 1 | bytes 8 | tf_op jit(solution)/shard_map/psum | solution.py:313
  268.6 3.3 fusion.80
  272.0 2.9 copy.294
  278.8 2.9 copy.296
  283.2 2.9 copy.295
  287.7 5.6 multiply_convert_fusion.2
  299.2 4.3 fusion.7
  324.0 3.8 copy.311
  327.8 5.3 convert_element_type.173
  333.1 3.8 fusion.144
  347.9 6.0 fusion.95
  353.9 5.4 reshape.409
  359.4 4.9 copy.315
  366.6 3.2 copy.314
  376.6 7.4 pad_maximum_fusion
  384.0 15.5 gather_fusion.1
  399.5 12.6 copy.316
  412.2 23.9 %reduce-scatter.5.cloned.1.call-done = f32[256,512]{1,0:T(8,128)} async-done(((f32[2048,512]{1,0:T(8,128)}), f32[256,512]{1,0:T(8,128)}) %reduce-scatter.5.cloned.1.call-update) | async-done | bytes 524304 | tf_op jit(solution)/shard_map/reduce_scatter | solution.py:428
  436.1 210.5 %reduce-scatter.3.cloned.1.call-done = f32[24,128,128]{1,2,0:T(8,128)} async-done(((f32[192,128,128]{1,2,0:T(8,128)}), f32[24,128,128]{1,2,0:T(8,128)}) %reduce-scatter.3.cloned.1.call-update) | async-done | bytes 1572880 | tf_op jit(solution)/shard_map/reduce_scatter | solution.py:427
  646.7 3.0 copy.339
  649.7 2.9 copy.336
  652.6 3.2 copy.337
  657.7 3.4 select_reduce_fusion
  667.6 39.6 %all-reduce = (f32[]{:T(128)}, f32[24,512]{1,0:T(8,128)S(1)}) all-reduce(f32[]{:T(128)S(6)} %div.165, f32[24,512]{1,0:T(8,128)S(1)} %concatenate.33), channel_id=1, replica_groups=mesh['dp'=4,'fsdp'=8] {'dp','fsdp'}, use_global_device_ids=true, to_apply=%region_24.26 | all-reduce | flops 12289 | bytes 98312 | tf_op jit(solution)/shard_map/psum | solution.py:431
  713.4 123.8 %all-reduce.5.cloned.1.call-done = f32[513,529]{0,1:T(8,128)} async-done(((f32[513,529]{0,1:T(8,128)}), f32[513,529]{0,1:T(8,128)}) %all-reduce.5.cloned.1.call-update) | async-done | bytes 1085524 | tf_op jit(solution)/shard_map/psum | solution.py:431
  839.5 21.5 %psum.53 = f32[]{:T(128)} all-reduce(f32[]{:T(128)S(6)} %add.312), channel_id=1, replica_groups=mesh['dp'=4,'fsdp'=8] {'fsdp'}, use_global_device_ids=true, to_apply=%region_38.40 | all-reduce | flops 1 | bytes 8 | tf_op jit(solution)/shard_map/psum | solution.py:434
  863.1 4.2 fusion.61
  872.1 4.5 multiply_subtract_fusion
  876.7 4.1 abs_reduce_fusion.1
  880.8 4.6 abs_reduce_fusion
  885.6 3.1 convolution_divide_fusion
  888.7 3.8 fusion.150
  892.5 3.0 copy.333
  895.6 3.3 fusion.36
  898.8 283.2 %custom-call.10 = f32[24,128,128]{2,1,0:T(8,128)} custom-call(f32[24,128,128]{2,1,0:T(8,128)} %fusion.36), custom_call_target="Cholesky" | custom-call | tf_op jit(solution)/shard_map/jit(cholesky)/cholesky | solution.py:235
  1182.1 3.5 convolution_divide_fusion.1
  1186.8 3.9 fusion.149
  1190.7 3.0 copy.329
  1193.7 3.3 fusion.40
  1197.0 283.0 %custom-call.8 = f32[24,128,128]{2,1,0:T(8,128)} custom-call(f32[24,128,128]{2,1,0:T(8,128)} %fusion.40), custom_call_target="Cholesky" | custom-call | tf_op jit(solution)/shard_map/jit(cholesky)/cholesky | solution.py:235
  1484.9 237.2 %custom-call.9 = f32[24,1,128,128]{2,3,1,0:T(8,128)} custom-call(f32[24,1,128,128]{3,2,1,0:T(8,128)} %get-tuple-element.179), custom_call_target="InvertDiagBlocksLowerTriangular" | custom-call | tf_op jit(solution)/shard_map/jit(_solve_triangular)/vmap()/triangular_solve | solution.py:236
  1722.1 5.7 fusion.47
  1727.7 3.0 copy.341
  1730.8 237.4 %custom-call.11 = f32[24,1,128,128]{2,3,1,0:T(8,128)} custom-call(f32[24,1,128,128]{3,2,1,0:T(8,128)} %get-tuple-element.178), custom_call_target="InvertDiagBlocksLowerTriangular" | custom-call | tf_op jit(solution)/shard_map/jit(_solve_triangular)/vmap()/triangular_solve | solution.py:236
  1968.2 5.2 fusion.52
  1973.4 3.0 copy.342
  1976.4 5.2 multiply_subtract_fusion.1
  1983.1 2.9 copy.344
  1986.0 2.9 copy.345
  1993.1 2.8 multiply_subtract_fusion.2
  (327 shorter events, 126.1 us)
Async XLA Ops:
  7.2 860.1 %copy-start = (f32[24,128,128]{2,1,0:T(8,128)S(1)}, f32[24,128,128]{2,1,0:T(8,128)}, u32[]{:S(2)}) copy-start(f32[24,128,128]{2,1,0:T(8,128)} %param.45) | copy-start | bytes 4718596
  7.2 55.5 %all-gather.3.cloned.1.call-start = ((), (), s32[]{:S(2)}) async-start(), calls=%async_computation.2 | async-start | bytes 2359296 | tf_op jit(solution)/shard_map/all_gather | solution.py:317
  9.2 2.6 copy-start.71
  9.2 2.8 copy-start.68
  9.2 3.0 copy-start.61
  9.2 3.3 copy-start.76
  9.2 3.3 copy-start.77
  9.2 153.5 %all-gather.5.cloned.1.call-start = ((), (), s32[]{:S(2)}) async-start(), calls=%async_computation.3 | async-start | bytes 7077888 | tf_op jit(solution)/shard_map/all_gather | solution.py:316
  11.7 424.3 %reduce-scatter.5.cloned.1.call-start = ((), (), s32[]{:S(2)}) async-start(), calls=%async_computation.5 | async-start | bytes 4718592 | tf_op jit(solution)/shard_map/reduce_scatter | solution.py:428
  16.8 3.2 copy-start.73
  16.8 3.3 copy-start.74
  16.8 3.4 copy-start.72
  22.2 2.9 copy-start.75
  22.2 6.9 copy-start.66
  31.0 31.7 %copy-start.64 = (pred[512,1024]{1,0:T(32,128)(4,1)}, pred[512,1024]{1,0:T(32,128)(4,1)S(1)}, u32[]{:S(2)}) copy-start(pred[512,1024]{1,0:T(32,128)(4,1)S(1)} %broadcast_compare_fusion) | copy-start | bytes 1572868
  62.7 2.1 copy-start.32
  66.1 118.7 %copy-start.38 = (bf16[512,512]{0,1:T(8,128)(2,1)}, bf16[512,512]{0,1:T(8,128)(2,1)S(1)}, u32[]{:S(2)}) copy-start(bf16[512,512]{0,1:T(8,128)(2,1)S(1)} %add_convert_fusion.2) | copy-start | bytes 1572868
  201.7 2.0 copy-start.15
  205.1 5.2 slice-start
  216.0 3.1 copy-start.26
  216.0 3.1 copy-start.50
  219.6 2.3 copy-start.9
  221.9 2.0 copy-start.78
  224.0 2.2 copy-start.7
  226.2 1.9 copy-start.5
  274.8 2.2 copy-start.4
  287.7 5.7 copy-start.41
  287.7 5.7 copy-start.42
  287.7 6.6 copy-start.63
  296.1 2.2 copy-start.79
  297.1 2.1 copy-start.46
  299.2 6.0 copy-start.35
  299.2 4.4 copy-start.10
  299.2 4.4 copy-start.44
  305.2 2.1 copy-start.51
  313.5 2.8 copy-start.2
  313.6 2.8 copy-start.16
  313.6 3.1 copy-start.17
  339.5 1.9 copy-start.37
  346.7 299.9 %reduce-scatter.3.cloned.1.call-start = ((), (), s32[]{:S(2)}) async-start(), calls=%async_computation.4 | async-start | bytes 14155776 | tf_op jit(solution)/shard_map/reduce_scatter | solution.py:427
  359.4 4.9 copy-start.11
  359.4 4.9 copy-start.53
  366.5 3.3 copy-start.27
  370.0 2.7 copy-start.48
  374.3 2.3 copy-start.6
  412.1 295.6 %all-reduce.7.cloned.1.call-start = ((), (), s32[]{:S(2)}) async-start(), calls=%async_computation.7 | async-start | bytes 4194304 | tf_op jit(solution)/shard_map/psum | solution.py:430
  646.6 190.6 %all-reduce.5.cloned.1.call-start = ((), (), s32[]{:S(2)}) async-start(), calls=%async_computation.6 | async-start | bytes 2744320 | tf_op jit(solution)/shard_map/psum | solution.py:431
  652.6 3.4 copy-start.25
  661.1 5.3 copy-start.62
  709.5 153.5 %copy-start.3 = (f32[24,128,128]{1,2,0:T(8,128)S(1)}, f32[24,128,128]{1,2,0:T(8,128)}, u32[]{:S(2)}) copy-start(f32[24,128,128]{1,2,0:T(8,128)} %get-tuple-element.142) | copy-start | bytes 4718596
  863.1 4.3 copy-start.54
  863.1 4.3 copy-start.55
  867.4 2.2 copy-start.56
  869.5 2.6 copy-start.57
  869.5 2.5 copy-start.58
  869.6 2.5 copy-start.20
  872.1 4.5 copy-start.59
  876.7 4.1 copy-start.60
  1480.0 2.6 copy-start.21
  1480.0 2.8 copy-start.22
  1988.9 4.2 copy-start.49
  1993.1 2.8 copy-start.67
  1993.1 2.8 copy-start.69
  1993.1 2.8 copy-start.70
  (23 other events, 31.5 us)
Sparse Core Ops, SparseCore 0:
  10.7 51.9 all-gather.2
  65.5 97.2 all-gather.4
  346.9 89.1 reduce-scatter.4
  439.5 207.0 reduce-scatter.2
  648.9 50.8 all-reduce.6
  705.5 131.6 all-reduce.4
where the time goes:
time: 2020 us; the launch traced here: 2000 us
  other arithmetic  1120 us (55%)
  waiting for transfers between devices  487 us (24%)
  local copies, waits for them, and re-layouts  182 us (9%)
  blocking collectives  100 us (5%)
  matrix products  95.5 us (5%)
  between operations  22.6 us (1%)
    another operation x6, other arithmetic, renew(): lower_factor = jnp.linalg.cholesky(gram)  569 us
    another operation x4, other arithmetic, renew(): jax.scipy.linalg.solve_triangular(lower_factor, jnp.swapaxes(iterate, 1,...  477 us
    reduce_scatter x1, waiting for transfers between devices, shards(): lax.psum_scatter(grad_slots, 'fsdp', scatter_dimension=0, tiled=True)  211 us
    psum x1, waiting for transfers between devices, shards(): lax.psum((head_local, small_local, loss_local), ('dp', 'fsdp'))  124 us
    all_gather x1, waiting for transfers between devices, shards(): lax.all_gather(shard_low[0], 'fsdp', axis=0, tiled=True)  96.7 us
    unnamed x175, local copies, waits for them, and re-layouts  46.4 us
  transfers between devices with their start and end apart: 6, of which 5 were waited for; matrix products, arithmetic and copies ran while one was open for 5% of the time, Pallas kernels for 0%

commit v1 on v0

--- a/solution.py
+++ b/solution.py
@@ -1,8 +1,11 @@
+import functools
 import math
 
 import jax
 import jax.numpy as jnp
 from jax import lax
+from jax.experimental import pallas as pl
+from jax.experimental.pallas import tpu as pltpu
 from jax.sharding import PartitionSpec as P
 
 D = 512
@@ -19,6 +22,8 @@
 NGAME = 26
 BS = 128
 STEP = 10
+PAN = 16
+PACK = 8
 
 
 HIGHEST = lax.Precision.HIGHEST
@@ -228,15 +233,96 @@
     return (-jnp.sum(log_probs * weights, -1), jnp.exp(log_probs) - weights)
 
 
-def renew(stat, basis):
-    scale = jnp.max(jnp.sum(jnp.abs(stat), -1), -1)[:, None, None]
-    iterate = jnp.einsum("bij,bjk->bik", stat, basis, precision=HIGHEST) / scale
-    gram = jnp.einsum("bji,bjk->bik", iterate, iterate, precision=HIGHEST)
-    lower_factor = jnp.linalg.cholesky(gram)
-    solved = jax.scipy.linalg.solve_triangular(
-        lower_factor, jnp.swapaxes(iterate, 1, 2), lower=True
-    )
-    return jnp.swapaxes(solved, 1, 2)
+def hdot(a, b, ca, cb):
+    return lax.dot_general(a, b, (((ca,), (cb,)), ((), ())), precision=HIGHEST, preferred_element_type=jnp.float32)
+
+def qr_kernel(count, stat_ref, basis_ref, out_ref, work):
+    tiles = -(-count // PACK)
+    rows = PACK * PAN
+    panels = BS // PAN
+
+    def start(b, _):
+        stat = stat_ref[b]
+        scale = jnp.max(jnp.sum(jnp.abs(stat), -1, keepdims=True), 0, keepdims=True)
+        xt = hdot(basis_ref[b], stat, 0, 0) / scale
+        gram = hdot(xt, xt, 1, 1)
+        for p in range(panels):
+            work[p, pl.ds(b * PAN, PAN), :BS] = gram[p * PAN : (p + 1) * PAN]
+            work[p, pl.ds(b * PAN, PAN), BS:] = xt[p * PAN : (p + 1) * PAN]
+        return _
+
+    lax.fori_loop(0, count, start, 0, unroll=2)
+    row_id = lax.broadcasted_iota(jnp.int32, (PAN, BS), 0)
+    lane_id = lax.broadcasted_iota(jnp.int32, (PAN, BS), 1)
+    group = lane_id // PAN
+    for p in range(panels):
+        packed = []
+        for t in range(tiles):
+            tile = jnp.zeros((PAN, BS), jnp.float32)
+            for c in range(PACK):
+                b = t * PACK + c
+                if b < count:
+                    diag = work[p, b * PAN : (b + 1) * PAN, :BS]
+                    shift = (c - p) * PAN % BS
+                    if shift:
+                        diag = pltpu.roll(diag, shift, 1)
+                    tile = jnp.where(group == c, diag, tile)
+                else:
+                    tile = jnp.where((group == c) & (lane_id % PAN == row_id), 1.0, tile)
+            packed.append(tile)
+        inverse = [jnp.where(lane_id % PAN == row_id, 1.0, 0.0) for _ in range(tiles)]
+        scales = [jnp.ones((PAN, BS), jnp.float32) for _ in range(tiles)]
+        for k in range(PAN):
+            index = group * PAN + k
+            for t in range(tiles):
+                tile = packed[t]
+                column = jnp.take_along_axis(tile, index, axis=1, mode="promise_in_bounds")
+                pivot = column[k : k + 1]
+                scales[t] = jnp.where(row_id == k, lax.rsqrt(pivot), scales[t])
+                if k < PAN - 1:
+                    factor = jnp.where(row_id > k, column * (1.0 / pivot), 0.0)
+                    packed[t] = tile - factor * tile[k : k + 1]
+                    inverse[t] = inverse[t] - factor * inverse[t][k : k + 1]
+        for t in range(tiles):
+            low = inverse[t] * scales[t]
+            spread = jnp.concatenate([jnp.where(group == c, low, 0.0) for c in range(PACK)], 0)
+            here = min(rows, (count - t * PACK) * PAN)
+            spread = spread[:here]
+            if here < rows:
+                spread = spread[:, :here]
+            span = slice(t * rows, t * rows + here)
+            work[p, span, :] = hdot(spread, work[p, span, :], 1, 0)
+        if p < panels - 1:
+
+            def trail(b, _, p=p):
+                upper = work[p, pl.ds(b * PAN, PAN), :]
+                lower = upper[:, :BS].T[(p + 1) * PAN :]
+                change = hdot(lower, upper, 1, 0)
+                for q in range(p + 1, panels):
+                    span = slice((q - p - 1) * PAN, (q - p) * PAN)
+                    work[q, pl.ds(b * PAN, PAN), :] -= change[span]
+                return _
+
+            lax.fori_loop(0, count, trail, 0, unroll=4 if count % 4 == 0 else 1)
+
+    def finish(b, _):
+        rows_q = jnp.concatenate([work[p, pl.ds(b * PAN, PAN), BS:] for p in range(panels)], 0)
+        out_ref[b] = rows_q.T
+        return _
+
+    lax.fori_loop(0, count, finish, 0, unroll=2)
+
+
+def renew_all(stats, bases):
+    count = stats.shape[0]
+    return pl.pallas_call(
+        functools.partial(qr_kernel, count),
+        out_shape=jax.ShapeDtypeStruct((count, BS, BS), jnp.float32),
+        in_specs=[pl.BlockSpec(memory_space=pltpu.VMEM)] * 2,
+        out_specs=pl.BlockSpec(memory_space=pltpu.VMEM),
+        scratch_shapes=[pltpu.VMEM((BS // PAN, count * PAN, 2 * BS), jnp.float32)],
+        name="renew",
+    )(stats, bases)
 
 
 def soap_update(weight, first_moment, second_moment, left, right, left_rot, right_rot, grad):
@@ -258,14 +344,18 @@
     direction = jnp.einsum("bij,bjk->bik", left_rot, direction, precision=HIGHEST)
     direction = jnp.einsum("bij,bkj->bik", direction, right_rot, precision=HIGHEST)
     weight = weight - learn_rate * (direction + weight_decay * weight)
+    count = weight.shape[0]
+    renewed = renew_all(
+        jnp.concatenate([left, right], 0), jnp.concatenate([left_rot, right_rot], 0)
+    )
     return (
         weight,
         first_moment,
         second_moment,
         left,
         right,
-        renew(left, left_rot),
-        renew(right, right_rot),
+        renewed[:count],
+        renewed[count:],
     )
 
 

time: 2020 us -> 1060 us (0.52)
  other arithmetic: 1120 us -> 63 us
  Pallas kernels: 0 us -> 149 us
  matrix products: 95.5 us -> 65.9 us
  local copies, waits for them, and re-layouts: 182 us -> 160 us
    another operation x10 -> x0, other arithmetic: 1050 us -> none  [the longest x6 569 us: renew(): lower_factor = jnp.linalg.cholesky(gram)]
    pallas_call x0 -> x1, Pallas kernels: none -> 149 us  [renew_all(): pl.pallas_call(functools.partial(qr_kernel, count), out_shape=jax.ShapeDt...]
    unnamed x175 -> x181, local copies, waits for them, and re-layouts: 46.4 us -> 32.8 us
  transfers between devices with their start and end apart: 6 -> 6, of which waited for: 5 -> 5; matrix products, arithmetic and copies ran while one was open for 5% -> 10% of each run, Pallas kernels for 0% -> 0%
where the time goes in v1:
time: 1060 us; the launch traced here: 1050 us
  waiting for transfers between devices  490 us (46%)
  local copies, waits for them, and re-layouts  160 us (15%)
  Pallas kernels  149 us (14%)
  blocking collectives  101 us (10%)
  matrix products  65.9 us (6%)
  other arithmetic  63 us (6%)
  between operations  22.8 us (2%)
    reduce_scatter x1, waiting for transfers between devices, shards(): lax.psum_scatter(grad_slots, 'fsdp', scatter_dimension=0, tiled=True)  211 us
    pallas_call x1, Pallas kernels, renew_all(): pl.pallas_call(functools.partial(qr_kernel, count), out_shape=jax.ShapeDt...  149 us
    psum x1, waiting for transfers between devices, shards(): lax.psum((head_local, small_local, loss_local), ('dp', 'fsdp'))  123 us
    all_gather x1, waiting for transfers between devices, shards(): lax.all_gather(shard_low[0], 'fsdp', axis=0, tiled=True)  96.7 us
    psum x1, blocking collectives, shards(): lax.psum((head_local, small_local, loss_local), ('dp', 'fsdp'))  40.1 us
    psum x1, blocking collectives, shards(): counted = lax.psum(jnp.sum(valid_steps.astype(jnp.float32)), ('dp', 'fsdp'))  39 us
    all_gather x1, waiting for transfers between devices, shards(): lax.all_gather(shard_low[1], 'fsdp', axis=0, tiled=True)  35.3 us
    unnamed x181, local copies, waits for them, and re-layouts  32.8 us
  transfers between devices with their start and end apart: 6, of which 5 were waited for; matrix products, arithmetic and copies ran while one was open for 10% of the time, Pallas kernels for 0%

profile of v1, /device:TPU:0, one launch (start us, length us, event | category | flops | bytes accessed | tf_op | source)
XLA Modules:
  0.0 1051.9 jit_solution(12458051199633612930)
XLA Ops:
  9.2 2.4 convert_element_type.149
  20.0 3.0 copy.178
  23.0 3.2 sort.17
  28.1 35.3 %all-gather.3.cloned.1.call-done = bf16[2048,512]{1,0:T(8,128)(2,1)} async-done(((bf16[256,512]{1,0:T(8,128)(2,1)}), bf16[2048,512]{1,0:T(8,128)(2,1)}) %all-gather.3.cloned.1.call-update) | async-done | bytes 2097168 | tf_op jit(solution)/shard_map/all_gather | solution.py:407
  63.4 2.1 fusion.52
  66.7 96.7 %all-gather.5.cloned.1.call-done = bf16[192,128,128]{2,1,0:T(8,128)(2,1)} async-done(((bf16[24,128,128]{2,1,0:T(8,128)(2,1)}), bf16[192,128,128]{2,1,0:T(8,128)(2,1)}) %all-gather.5.cloned.1.call-update) | async-done | bytes 6291472 | tf_op jit(solution)/shard_map/all_gather | solution.py:406
  163.4 10.8 %gather_fusion = bf16[192,128,128]{2,1,0:T(8,128)(2,1)} fusion(bf16[192,128,128]{2,1,0:T(8,128)(2,1)} %all-gather.5.cloned.1.call-done, s32[1024]{0:T(1024)S(1)} %pad_clamp_fusion.1), kind=kCustom, calls=%fused_computation | custom fusion | bytes 12583680 | tf_op jit(solution)/shard_map/gather | solution.py:410
  176.1 4.9 fusion.118
  181.0 2.2 copy.182
  183.2 2.4 convolution_convert_fusion
  185.6 3.2 reshape.381
  188.8 3.5 fusion.120
  193.7 2.2 fusion.124
  198.6 2.4 copy.187
  201.0 2.6 reshape.382
  203.5 2.2 copy.188
  205.8 4.7 copy.190
  210.5 3.0 copy.189
  224.1 39.0 %psum.49 = f32[]{:T(128)} all-reduce(f32[]{:T(128)} %get-tuple-element.113), channel_id=1, replica_groups=mesh['dp'=4,'fsdp'=8] {'dp','fsdp'}, use_global_device_ids=true, to_apply=%region_23.25 | all-reduce | flops 1 | bytes 8 | tf_op jit(solution)/shard_map/psum | solution.py:403
  263.1 3.5 fusion.62
  266.6 3.0 copy.191
  269.5 2.1 bitcast_reduce_fusion
  273.6 2.9 copy.193
  278.1 2.9 copy.192
  282.6 5.6 multiply_convert_fusion.2
  294.1 4.3 fusion.7
  303.5 2.4 reshape.393
  305.9 2.6 copy.205
  308.5 2.0 convolution_bitcast_fusion.1
  315.2 2.1 fusion.130
  318.1 3.8 copy.208
  321.9 5.3 convert_element_type.173
  327.2 3.8 fusion.127
  336.8 2.4 pad_maximum_fusion.1
  340.4 6.0 fusion.77
  346.4 5.4 reshape.398
  351.9 4.9 copy.212
  359.0 3.2 copy.211
  368.8 7.4 pad_maximum_fusion
  376.3 15.5 %gather_fusion.1 = f32[192,128,128]{2,1,0:T(8,128)} fusion(f32[192,128,128]{2,1,0:T(8,128)} %pad_maximum_fusion, s32[1024]{0:T(1024)S(1)} %pad_clamp_fusion), kind=kCustom, calls=%fused_computation.1 | custom fusion | bytes 25166592 | tf_op jit(solution)/shard_map/gather | solution.py:510
  391.7 12.6 %copy.213 = f32[192,128,128]{1,2,0:T(8,128)} copy(f32[192,128,128]{2,1,0:T(8,128)} %gather_fusion.1) | data formatting | bytes 25165824 | tf_op jit(solution)/shard_map/gather | solution.py:510
  404.4 24.1 %reduce-scatter.5.cloned.1.call-done = f32[256,512]{1,0:T(8,128)} async-done(((f32[2048,512]{1,0:T(8,128)}), f32[256,512]{1,0:T(8,128)}) %reduce-scatter.5.cloned.1.call-update) | async-done | bytes 524304 | tf_op jit(solution)/shard_map/reduce_scatter | solution.py:518
  428.5 210.6 %reduce-scatter.3.cloned.1.call-done = f32[24,128,128]{1,2,0:T(8,128)} async-done(((f32[192,128,128]{1,2,0:T(8,128)}), f32[24,128,128]{1,2,0:T(8,128)}) %reduce-scatter.3.cloned.1.call-update) | async-done | bytes 1572880 | tf_op jit(solution)/shard_map/reduce_scatter | solution.py:517
  640.7 3.0 copy.223
  643.7 2.9 copy.224
  646.6 3.4 pad_maximum_fusion.3.basis_ref
  651.9 3.0 select_reduce_fusion
  660.2 40.1 %all-reduce = (f32[]{:T(128)}, f32[24,512]{1,0:T(8,128)S(1)}) all-reduce(f32[]{:T(128)S(6)} %div.135, f32[24,512]{1,0:T(8,128)S(1)} %concatenate.39), channel_id=1, replica_groups=mesh['dp'=4,'fsdp'=8] {'dp','fsdp'}, use_global_device_ids=true, to_apply=%region_24.26 | all-reduce | flops 12289 | bytes 98312 | tf_op jit(solution)/shard_map/psum | solution.py:521
  702.8 2.5 multiply_reduce_fusion.1
  706.6 123.1 %all-reduce.5.cloned.1.call-done = f32[513,529]{0,1:T(8,128)} async-done(((f32[513,529]{0,1:T(8,128)}), f32[513,529]{0,1:T(8,128)}) %all-reduce.5.cloned.1.call-update) | async-done | bytes 1085524 | tf_op jit(solution)/shard_map/psum | solution.py:521
  829.7 2.3 multiply_reduce_fusion.2
  832.0 21.5 %psum.53 = f32[]{:T(128)} all-reduce(f32[]{:T(128)S(6)} %add.303), channel_id=1, replica_groups=mesh['dp'=4,'fsdp'=8] {'fsdp'}, use_global_device_ids=true, to_apply=%region_38.40 | all-reduce | flops 1 | bytes 8 | tf_op jit(solution)/shard_map/psum | solution.py:524
  855.6 2.7 fusion.43
  858.3 2.2 multiply_add_fusion.2
  860.6 2.5 fusion.33
  863.1 4.6 multiply_subtract_fusion
  867.7 2.9 multiply_add_fusion.1
  870.6 3.4 multiply_add_fusion
  875.2 2.0 pad_maximum_fusion.2.stat_ref
  877.2 149.4 %renew.1 = f32[48,128,128]{2,1,0:T(8,128)} custom-call(f32[48,128,128]{2,1,0:T(8,128)} %pad_maximum_fusion.2.stat_ref, f32[48,128,128]{2,1,0:T(8,128)} %pad_maximum_fusion.3.basis_ref), custom_call_target="tpu_custom_call" | custom-call | tf_op jit(solution)/shard_map/renew/pallas_call | solution.py:318
  1026.6 4.0 fusion.119
  1030.6 2.2 multiply_subtract_fusion.1
  1034.3 2.9 copy.229
  1040.0 2.8 multiply_subtract_fusion.2
  (315 shorter events, 81.4 us)
Async XLA Ops:
  7.2 4.5 copy-start.75
  7.2 4.6 copy-start.72
  7.2 4.8 copy-start.66
  7.2 56.2 %all-gather.3.cloned.1.call-start = ((), (), s32[]{:S(2)}) async-start(), calls=%async_computation.2 | async-start | bytes 2359296 | tf_op jit(solution)/shard_map/all_gather | solution.py:407
  9.1 3.3 copy-start.80
  9.1 3.3 copy-start.81
  9.1 154.3 %all-gather.5.cloned.1.call-start = ((), (), s32[]{:S(2)}) async-start(), calls=%async_computation.3 | async-start | bytes 7077888 | tf_op jit(solution)/shard_map/all_gather | solution.py:406
  11.6 416.9 %reduce-scatter.5.cloned.1.call-start = ((), (), s32[]{:S(2)}) async-start(), calls=%async_computation.5 | async-start | bytes 4718592 | tf_op jit(solution)/shard_map/reduce_scatter | solution.py:518
  15.7 2.2 copy-start.77
  15.7 2.3 copy-start.78
  15.7 2.4 copy-start.76
  20.0 3.0 copy-start.79
  20.0 7.0 copy-start.70
  66.7 116.4 %copy-start.45 = (bf16[512,512]{0,1:T(8,128)(2,1)}, bf16[512,512]{0,1:T(8,128)(2,1)S(1)}, u32[]{:S(2)}) copy-start(bf16[512,512]{0,1:T(8,128)(2,1)S(1)} %add_convert_fusion.2) | copy-start | bytes 1572868
  176.1 4.9 slice-start
  210.5 3.1 copy-start.33
  210.5 3.1 copy-start.56
  214.1 2.3 copy-start.7
  218.4 2.2 copy-start.5
  269.5 2.2 copy-start.2
  282.6 5.7 copy-start.47
  282.6 5.7 copy-start.48
  282.6 6.6 copy-start.68
  289.1 2.8 copy-start.31
  291.0 2.2 copy-start.83
  291.9 2.1 copy-start.52
  294.1 6.0 copy-start.41
  294.1 4.4 copy-start.8
  294.1 4.4 copy-start.50
  300.1 2.1 copy-start.57
  339.2 299.9 %reduce-scatter.3.cloned.1.call-start = ((), (), s32[]{:S(2)}) async-start(), calls=%async_computation.4 | async-start | bytes 14155776 | tf_op jit(solution)/shard_map/reduce_scatter | solution.py:517
  351.9 4.9 copy-start.9
  351.9 4.9 copy-start.59
  359.0 3.3 copy-start.34
  359.0 4.3 copy-start.25
  362.3 2.6 copy-start.54
  363.3 3.2 copy-start.46
  366.5 2.3 copy-start.4
  404.4 234.8 %copy-start.16 = (f32[513,529]{1,0:T(8,128)S(1)}, f32[513,529]{1,0:T(8,128)}, u32[]{:S(2)}) copy-start(f32[513,529]{1,0:T(8,128)} %param.46) | copy-start | bytes 3256528
  404.4 296.5 %all-reduce.7.cloned.1.call-start = ((), (), s32[]{:S(2)}) async-start(), calls=%async_computation.7 | async-start | bytes 4194304 | tf_op jit(solution)/shard_map/psum | solution.py:520
  639.1 190.6 %all-reduce.5.cloned.1.call-start = ((), (), s32[]{:S(2)}) async-start(), calls=%async_computation.6 | async-start | bytes 2744320 | tf_op jit(solution)/shard_map/psum | solution.py:521
  640.7 5.9 copy-start.10
  646.6 3.5 copy-start.32
  651.9 3.0 copy-start.40
  654.9 4.2 copy-start.67
  659.1 196.5 %copy-start.21 = (f32[24,128,128]{2,1,0:T(8,128)S(1)}, f32[24,128,128]{2,1,0:T(8,128)}, u32[]{:S(2)}) copy-start(f32[24,128,128]{2,1,0:T(8,128)} %param.41) | copy-start | bytes 4718596
  700.9 154.7 %copy-start.1 = (f32[24,128,128]{1,2,0:T(8,128)S(1)}, f32[24,128,128]{1,2,0:T(8,128)}, u32[]{:S(2)}) copy-start(f32[24,128,128]{1,2,0:T(8,128)} %get-tuple-element.119) | copy-start | bytes 4718596
  855.6 2.7 copy-start.11
  855.6 2.7 copy-start.60
  855.6 2.7 copy-start.61
  860.5 2.5 copy-start.64
  860.6 2.5 copy-start.65
  860.6 2.5 copy-start.24
  863.1 4.6 copy-start.62
  867.7 2.9 copy-start.63
  870.6 3.4 copy-start.22
  1026.6 4.1 copy-start.27
  1026.6 4.1 copy-start.28
  1026.6 4.1 copy-start.29
  1026.6 4.1 copy-start.30
  1034.3 4.5 copy-start.44
  1040.0 2.8 copy-start.71
  1040.0 2.8 copy-start.73
  1040.0 2.8 copy-start.74
  (27 other events, 39.2 us)
Sparse Core Ops, SparseCore 0:
  10.7 52.6 all-gather.2
  66.1 97.2 all-gather.4
  339.3 89.1 reduce-scatter.4
  432.0 207.0 reduce-scatter.2
  641.4 50.8 all-reduce.6
  698.0 131.6 all-reduce.4
